TPU v7x, 32 devices: a whole 2x2x4 slice. The times are simulated.
32 devices in a mesh: groups: 2 (over x), tokens: 16 (over z, y, core).
Axes of the slice: x: 2, y: 2, z: 4, core: 2. Of those that a mesh axis runs over, the one named last changes fastest.
Arguments:
- text_query: bfloat16 [256, 2, 1280], P(('groups', 'tokens')), parts along dimension 0, may hold values from -6 to 6
- frame_key: bfloat16 [16384, 2, 1280], P(('groups', 'tokens')), parts along dimension 0, may hold values from -6 to 6
- frame_value: bfloat16 [16384, 2560], P(('groups', 'tokens')), parts along dimension 0, may hold values from -6 to 6
- forward_out: bfloat16 [256, 2, 2560], P(('groups', 'tokens')), parts along dimension 0, may hold values from -3 to 3
- out_grad: bfloat16 [256, 2560], P(('groups', 'tokens')), parts along dimension 0, may hold values from -1536 to 1536
- log_norms: float32 [256, 2, 10], P(('groups', 'tokens')), parts along dimension 0, as said below
- lambdas: float32 [10], replicated, may hold values from 0.2 to 0.8
- visits: int32 [32, 12], P('groups'), parts along dimension 0, may hold values from 0 to 15, all different within a row; in each aligned block of 16 rows (0 to 15, 16 to 31, ...) at most 14 rows name the same one
- bounds: int32 [32], P('groups'), parts along dimension 0, may hold values from 2 to 6, as said below
- text_count: int32 [1], replicated, may hold values from 64 to 128
Outputs:
- query_grad: bfloat16 [256, 2, 1280], P(('groups', 'tokens')), parts along dimension 0
- key_grad: bfloat16 [16384, 2, 1280], P(('groups', 'tokens')), parts along dimension 0
- value_grad: bfloat16 [16384, 2560], P(('groups', 'tokens')), parts along dimension 0
There are 2 independent parts, one for each index of `groups`. A program takes and returns all parts, laid end to end along the dimension named above; an argument that names none is the same for every part. Nothing has to cross between parts.
Inputs may be any that keep to these rules, and one draw needn't show every extreme that they name: `visits`: row b lists 6 frame shards for the first segment of text block b and then 6 for its second, all 12 different; every shard is listed by at most 14 blocks, a bound that some block reaches. Segment 1 of text block b begins at its row bounds[b]; some block has bounds 2 and some has 6, so no segment is longer than 6 rows. Text rows from text_count onward are padding in every group. `log_norms`: each entry lies within 1.5 of the logarithm of 3072.
All inputs are finite; a program needn't handle non-finite values.
Results may differ from a plain program's by a relative error of at most 0.005.
Values may be sent and summed in bfloat16 or wider, within the bound.
A program may use at most 128 MiB of HBM per device.

v0:
```python
import jax
import jax.numpy as jnp
from jax import lax
from jax.sharding import PartitionSpec as P


def segment_slots(in_first, in_second, bound_vals, block_ids, capacity, text_rows, text_count):
    start_row = jnp.where(in_second, bound_vals, 0)
    seg_length = jnp.where(in_first, bound_vals, jnp.where(in_second, text_rows - bound_vals, 0))
    slot_index = jnp.arange(capacity, dtype=jnp.int32)
    local_rows = start_row[:, None] + slot_index[None, :]
    global_rows = block_ids[:, None] * text_rows + local_rows
    used = jnp.logical_and(slot_index[None, :] < seg_length[:, None], global_rows < text_count[0])
    safe_rows = jnp.minimum(local_rows, text_rows - 1)
    return (safe_rows, used.astype(jnp.float32))


def place_rows(local_rows, used, text_rows):
    row_ids = jnp.arange(text_rows, dtype=jnp.int32)
    return (local_rows[:, :, None] == row_ids[None, None, :]).astype(jnp.float32) * used[:, :, None]


def visit_rows(
    query_rows,
    grad_rows,
    norm_rows,
    slope_rows,
    live_mask,
    frame_key,
    frame_value,
    lambdas,
    key_acc,
    value_acc,
):
    head_count = lambdas.shape[0]
    key_size = frame_key.shape[2] // head_count
    value_size = frame_value.shape[1] // head_count
    score_scale = float(key_size) ** (-0.5)
    part_rows = query_rows.shape[0]

    def head_step(head_index, running):
        key_total, value_total, query_part = running
        q_head = lax.dynamic_slice_in_dim(query_rows, head_index * key_size, key_size, 2)
        k_head = lax.dynamic_slice_in_dim(frame_key, head_index * key_size, key_size, 2)
        v_head = lax.dynamic_slice_in_dim(frame_value, head_index * value_size, value_size, 1)
        g_head = lax.dynamic_slice_in_dim(grad_rows, head_index * value_size, value_size, 1)
        norm_head = lax.dynamic_index_in_dim(norm_rows, head_index, 2, keepdims=False)
        slope_head = lax.dynamic_index_in_dim(slope_rows, head_index, 2, keepdims=False)
        weight_two = lax.dynamic_index_in_dim(lambdas, head_index, 0, keepdims=False)
        spread = jnp.dot(g_head, v_head.T, preferred_element_type=jnp.float32)
        score_one = (
            jnp.dot(q_head[:, 0], k_head[:, 0].T, preferred_element_type=jnp.float32) * score_scale
        )
        score_two = (
            jnp.dot(q_head[:, 1], k_head[:, 1].T, preferred_element_type=jnp.float32) * score_scale
        )
        prob_one = live_mask[:, None] * jnp.exp(score_one - norm_head[:, 0:1])
        prob_two = live_mask[:, None] * jnp.exp(score_two - norm_head[:, 1:2])
        grad_one = (prob_one * (spread - slope_head[:, 0:1])).astype(jnp.bfloat16)
        grad_two = (prob_two * (-weight_two * spread - slope_head[:, 1:2])).astype(jnp.bfloat16)
        mixed_weight = (prob_one - weight_two * prob_two).astype(jnp.bfloat16)
        value_new = jnp.dot(mixed_weight.T, g_head, preferred_element_type=jnp.float32)
        key_new = (
            jnp.stack(
                [
                    jnp.dot(grad_one.T, q_head[:, 0], preferred_element_type=jnp.float32),
                    jnp.dot(grad_two.T, q_head[:, 1], preferred_element_type=jnp.float32),
                ],
                axis=1,
            )
            * score_scale
        )
        query_new = (
            jnp.stack(
                [
                    jnp.dot(grad_one, k_head[:, 0], preferred_element_type=jnp.float32),
                    jnp.dot(grad_two, k_head[:, 1], preferred_element_type=jnp.float32),
                ],
                axis=1,
            )
            * score_scale
        )
        key_old = lax.dynamic_slice_in_dim(key_total, head_index * key_size, key_size, 2)
        key_total = lax.dynamic_update_slice_in_dim(
            key_total, key_old + key_new, head_index * key_size, 2
        )
        value_old = lax.dynamic_slice_in_dim(value_total, head_index * value_size, value_size, 1)
        value_total = lax.dynamic_update_slice_in_dim(
            value_total, value_old + value_new, head_index * value_size, 1
        )
        query_part = lax.dynamic_update_slice_in_dim(
            query_part, query_new, head_index * key_size, 2
        )
        return (key_total, value_total, query_part)

    query_start = jnp.zeros((part_rows,) + query_rows.shape[1:], jnp.float32)
    return lax.fori_loop(0, head_count, head_step, (key_acc, value_acc, query_start))


def per_device(
    text_query,
    frame_key,
    frame_value,
    forward_out,
    out_grad,
    log_norms,
    lambdas,
    visits,
    bounds,
    text_count,
):
    shard_count = lax.axis_size("tokens")
    my_index = lax.axis_index("tokens")
    text_rows = text_query.shape[0]
    head_count = lambdas.shape[0]
    value_size = frame_value.shape[1] // head_count
    visit_width = visits.shape[1] // 2
    capacity = 3 * text_rows // 4
    grads_wide = out_grad.astype(jnp.float32).reshape(text_rows, head_count, value_size)
    outs_wide = forward_out.astype(jnp.float32).reshape(text_rows, 2, head_count, value_size)
    map_coefs = jnp.stack([jnp.ones_like(lambdas), -lambdas])
    slopes = jnp.sum(grads_wide[:, None] * outs_wide, axis=3) * map_coefs[None]
    all_norms, all_slopes = (
        lax.all_gather(log_norms, "tokens", axis=0, tiled=True),
        lax.all_gather(slopes, "tokens", axis=0, tiled=True),
    )
    zero_keys = jnp.zeros(frame_key.shape, jnp.float32)
    zero_values = jnp.zeros(frame_value.shape, jnp.float32)
    shards = jnp.arange(shard_count, dtype=jnp.int32)
    query_shape = text_query.shape[1:]
    flat_width = query_shape[0] * query_shape[1]
    my_list = lax.dynamic_index_in_dim(visits, my_index, 0, keepdims=False)
    my_bound = lax.dynamic_index_in_dim(bounds, my_index, 0, keepdims=False)
    send_first = jnp.any(my_list[:visit_width][None, :] == shards[:, None], axis=1)
    send_second = jnp.any(my_list[visit_width:][None, :] == shards[:, None], axis=1)
    send_rows, send_used = segment_slots(
        send_first,
        send_second,
        jnp.broadcast_to(my_bound, (shard_count,)),
        jnp.broadcast_to(my_index, (shard_count,)),
        capacity,
        text_rows,
        text_count,
    )
    recv_first = jnp.any(visits[:, :visit_width] == my_index, axis=1)
    recv_second = jnp.any(visits[:, visit_width:] == my_index, axis=1)
    recv_rows, recv_used = segment_slots(
        recv_first, recv_second, bounds, shards, capacity, text_rows, text_count
    )
    flat_send = send_rows.reshape(-1)
    sent_query = jnp.take(text_query, flat_send, axis=0)
    sent_grad = jnp.take(out_grad, flat_send, axis=0)
    got_query, got_grad = (
        lax.all_to_all(sent_query, "tokens", split_axis=0, concat_axis=0, tiled=True),
        lax.all_to_all(sent_grad, "tokens", split_axis=0, concat_axis=0, tiled=True),
    )
    global_recv = (shards[:, None] * text_rows + recv_rows).reshape(-1)
    norm_rows = jnp.take(all_norms, global_recv, axis=0)
    slope_rows = jnp.take(all_slopes, global_recv, axis=0)
    key_acc, value_acc, query_part = visit_rows(
        got_query,
        got_grad,
        norm_rows,
        slope_rows,
        recv_used.reshape(-1),
        frame_key,
        frame_value,
        lambdas,
        zero_keys,
        zero_values,
    )
    came_back = lax.all_to_all(query_part, "tokens", split_axis=0, concat_axis=0, tiled=True)
    grouped = came_back.reshape(shard_count, came_back.shape[0] // shard_count, flat_width)
    placing = place_rows(send_rows, send_used, text_rows)
    query_sum = jnp.einsum(
        "jsx,jsc->xc", placing, grouped, precision=lax.Precision.HIGHEST
    ).reshape((text_rows,) + query_shape)
    return (
        query_sum.astype(jnp.bfloat16),
        key_acc.astype(jnp.bfloat16),
        value_acc.astype(jnp.bfloat16),
    )


def solution(mesh):
    return jax.shard_map(
        per_device,
        mesh=mesh,
        in_specs=(
            P(("groups", "tokens"), None, None),
            P(("groups", "tokens"), None, None),
            P(("groups", "tokens"), None),
            P(("groups", "tokens"), None, None),
            P(("groups", "tokens"), None),
            P(("groups", "tokens"), None, None),
            P(),
            P("groups", None),
            P("groups"),
            P(),
        ),
        out_specs=(
            P(("groups", "tokens"), None, None),
            P(("groups", "tokens"), None, None),
            P(("groups", "tokens"), None),
        ),
        check_vma=False,
    )
```

profile of v0, /device:TPU:9, one launch (start us, length us, event | category | flops | bytes accessed | tf_op | source)
XLA Modules:
  0.0 243.4 jit_solution(16591408216141167793)
XLA Ops:
  1.4 1.2 dynamic_slice.74
  5.0 2.1 gather_fusion.1
  8.4 6.6 %all-to-all-start.1 = ((bf16[16,6,2560]{2,1,0:T(8,128)(2,1)}), bf16[16,6,2560]{2,1,0:T(8,128)(2,1)S(1)}, u32[]{:S(2)}, u32[]{:S(2)}) async-start(bf16[16,6,2560]{2,1,0:T(8,128)(2,1)} %broadcast_select_fusion.1), calls=%async_computation.1 | async-start | bytes 1310720 | tf_op jit(solution)/shard_map/all_to_all | solution.py:155
  15.6 1.6 gather_fusion
  17.3 1.3 broadcast_select_fusion
  18.7 13.2 %all-to-all-done.1 = bf16[16,6,2560]{2,1,0:T(8,128)(2,1)S(1)} async-done(((bf16[16,6,2560]{2,1,0:T(8,128)(2,1)}), bf16[16,6,2560]{2,1,0:T(8,128)(2,1)S(1)}, u32[]{:S(2)}, u32[]{:S(2)}) %all-to-all-start.1) | async-done | bytes 491552 | tf_op jit(solution)/shard_map/all_to_all | solution.py:155
  31.9 4.5 %all-to-all-start = ((bf16[96,2,1280]{2,1,0:T(2,128)(2,1)}), bf16[96,2,1280]{2,1,0:T(2,128)(2,1)S(1)}, u32[]{:S(2)}, u32[]{:S(2)}) async-start(bf16[96,2,1280]{2,1,0:T(2,128)(2,1)} %broadcast_select_fusion), calls=%async_computation | async-start | bytes 983040 | tf_op jit(solution)/shard_map/all_to_all | solution.py:154
  36.4 23.7 %all_gather.6 = f32[128,2,10]{2,1,0:T(2,128)S(1)} all-gather(f32[8,2,10]{2,1,0:T(2,128)S(1)} %copy-done.4), channel_id=1, replica_groups=mesh['groups'=2,'tokens'=16] {'tokens'}, dimensions={0}, use_global_device_ids=true | all-gather | bytes 10880 | tf_op jit(solution)/shard_map/all_gather | solution.py:124
  60.8 17.2 %all_gather.7 = f32[128,2,10]{2,1,0:T(2,128)S(1)} all-gather(f32[8,2,10]{2,1,0:T(2,128)S(1)} %copy.61), channel_id=1, replica_groups=mesh['groups'=2,'tokens'=16] {'tokens'}, dimensions={0}, use_global_device_ids=true | all-gather | bytes 10880 | tf_op jit(solution)/shard_map/all_gather | solution.py:125
  79.3 1.2 broadcast_in_dim.73.clone
  80.5 3.0 %broadcast_in_dim.72 = f32[512,2560]{1,0:T(8,128)} broadcast(f32[]{:T(128)} %constant.125.clone.1), dimensions={} | broadcast | bytes 5242884 | tf_op jit(solution)/shard_map/broadcast_in_dim | solution.py:128
  83.5 3.6 %broadcast_in_dim.71.clone = f32[512,2,1280]{2,1,0:T(2,128)} broadcast(f32[]{:T(128)} %constant.125.clone.1), dimensions={} | broadcast | bytes 5242884 | tf_op jit(solution)/shard_map/broadcast_in_dim | solution.py:127
  87.1 122.9 %while.18 = (s32[]{:T(128)}, f32[512,2,1280]{2,1,0:T(2,128)}, f32[512,2560]{1,0:T(8,128)}, f32[96,2,1280]{2,1,0:T(2,128)}, bf16[96,2,1280]{2,1,0:T(2,128)(2,1)S(...) while((s32[]{:T(128)}, f32[512,2,1280]{2,1,0:T(2,128)}, ...), condition=%wide.region_6.8_spmd.clone, body=%wide.region_5.7_spmd.clone.sunk | while | flops 127189576 | bytes 9318833 | solution.py:97
  89.3 1.2 fusion.61
  90.5 1.6 constant_dynamic-slice_fusion.11
  93.4 1.1 constant_dynamic-slice_fusion.13
  95.3 1.3 copy_dynamic-update-slice_fusion.4
  96.5 2.8 %fusion.66 = f32[512,2560]{1,0:T(8,128)} fusion(f32[512,2560]{1,0:T(8,128)} %get-tuple-element.518, s32[]{:T(128)S(6)} %select_n.149, f32[96,512]{1,0:T(8,128)S(1)} %get-tuple-element.493, f32[96,512]{1,0:T(8,128)S(1)} %fusion.64, f32[]{:T(128)} %bitcast.109, bf16[96,2560]{1,0:T(8,128)(2,1)S(1)} %get-tuple-element.545), kind=kOutput, calls=%fused_computation.6.clone.1 | convolution fusion | flops 25444352 | bytes 1492480 | tf_op jit(solution)/shard_map/while/body/eval_jaxpr/dot_general | solution.py:62
  101.6 1.2 fusion.61
  102.7 1.6 constant_dynamic-slice_fusion.11
  105.6 1.1 constant_dynamic-slice_fusion.13
  107.5 1.3 copy_dynamic-update-slice_fusion.4
  108.8 2.9 %fusion.66 = f32[512,2560]{1,0:T(8,128)} fusion(f32[512,2560]{1,0:T(8,128)} %get-tuple-element.518, s32[]{:T(128)S(6)} %select_n.149, f32[96,512]{1,0:T(8,128)S(1)} %get-tuple-element.493, f32[96,512]{1,0:T(8,128)S(1)} %fusion.64, f32[]{:T(128)} %bitcast.109, bf16[96,2560]{1,0:T(8,128)(2,1)S(1)} %get-tuple-element.545), kind=kOutput, calls=%fused_computation.6.clone.1 | convolution fusion | flops 25444352 | bytes 1492480 | tf_op jit(solution)/shard_map/while/body/eval_jaxpr/dot_general | solution.py:62
  113.9 1.2 fusion.61
  115.1 1.7 constant_dynamic-slice_fusion.11
  118.0 1.1 constant_dynamic-slice_fusion.13
  119.9 1.3 copy_dynamic-update-slice_fusion.4
  121.2 2.8 %fusion.66 = f32[512,2560]{1,0:T(8,128)} fusion(f32[512,2560]{1,0:T(8,128)} %get-tuple-element.518, s32[]{:T(128)S(6)} %select_n.149, f32[96,512]{1,0:T(8,128)S(1)} %get-tuple-element.493, f32[96,512]{1,0:T(8,128)S(1)} %fusion.64, f32[]{:T(128)} %bitcast.109, bf16[96,2560]{1,0:T(8,128)(2,1)S(1)} %get-tuple-element.545), kind=kOutput, calls=%fused_computation.6.clone.1 | convolution fusion | flops 25444352 | bytes 1492480 | tf_op jit(solution)/shard_map/while/body/eval_jaxpr/dot_general | solution.py:62
  126.2 1.2 fusion.61
  127.3 1.7 constant_dynamic-slice_fusion.11
  130.3 1.1 constant_dynamic-slice_fusion.13
  132.2 1.3 copy_dynamic-update-slice_fusion.4
  133.5 2.8 %fusion.66 = f32[512,2560]{1,0:T(8,128)} fusion(f32[512,2560]{1,0:T(8,128)} %get-tuple-element.518, s32[]{:T(128)S(6)} %select_n.149, f32[96,512]{1,0:T(8,128)S(1)} %get-tuple-element.493, f32[96,512]{1,0:T(8,128)S(1)} %fusion.64, f32[]{:T(128)} %bitcast.109, bf16[96,2560]{1,0:T(8,128)(2,1)S(1)} %get-tuple-element.545), kind=kOutput, calls=%fused_computation.6.clone.1 | convolution fusion | flops 25444352 | bytes 1492480 | tf_op jit(solution)/shard_map/while/body/eval_jaxpr/dot_general | solution.py:62
  138.5 1.2 fusion.61
  139.7 1.6 constant_dynamic-slice_fusion.11
  142.5 1.1 constant_dynamic-slice_fusion.13
  144.5 1.2 copy_dynamic-update-slice_fusion.4
  145.7 2.8 %fusion.66 = f32[512,2560]{1,0:T(8,128)} fusion(f32[512,2560]{1,0:T(8,128)} %get-tuple-element.518, s32[]{:T(128)S(6)} %select_n.149, f32[96,512]{1,0:T(8,128)S(1)} %get-tuple-element.493, f32[96,512]{1,0:T(8,128)S(1)} %fusion.64, f32[]{:T(128)} %bitcast.109, bf16[96,2560]{1,0:T(8,128)(2,1)S(1)} %get-tuple-element.545), kind=kOutput, calls=%fused_computation.6.clone.1 | convolution fusion | flops 25444352 | bytes 1492480 | tf_op jit(solution)/shard_map/while/body/eval_jaxpr/dot_general | solution.py:62
  150.8 1.2 fusion.61
  151.9 1.7 constant_dynamic-slice_fusion.11
  154.9 1.1 constant_dynamic-slice_fusion.13
  156.8 1.3 copy_dynamic-update-slice_fusion.4
  158.1 2.8 %fusion.66 = f32[512,2560]{1,0:T(8,128)} fusion(f32[512,2560]{1,0:T(8,128)} %get-tuple-element.518, s32[]{:T(128)S(6)} %select_n.149, f32[96,512]{1,0:T(8,128)S(1)} %get-tuple-element.493, f32[96,512]{1,0:T(8,128)S(1)} %fusion.64, f32[]{:T(128)} %bitcast.109, bf16[96,2560]{1,0:T(8,128)(2,1)S(1)} %get-tuple-element.545), kind=kOutput, calls=%fused_computation.6.clone.1 | convolution fusion | flops 25444352 | bytes 1492480 | tf_op jit(solution)/shard_map/while/body/eval_jaxpr/dot_general | solution.py:62
  163.1 1.2 fusion.61
  164.3 1.7 constant_dynamic-slice_fusion.11
  167.2 1.1 constant_dynamic-slice_fusion.13
  169.1 1.3 copy_dynamic-update-slice_fusion.4
  170.4 2.8 %fusion.66 = f32[512,2560]{1,0:T(8,128)} fusion(f32[512,2560]{1,0:T(8,128)} %get-tuple-element.518, s32[]{:T(128)S(6)} %select_n.149, f32[96,512]{1,0:T(8,128)S(1)} %get-tuple-element.493, f32[96,512]{1,0:T(8,128)S(1)} %fusion.64, f32[]{:T(128)} %bitcast.109, bf16[96,2560]{1,0:T(8,128)(2,1)S(1)} %get-tuple-element.545), kind=kOutput, calls=%fused_computation.6.clone.1 | convolution fusion | flops 25444352 | bytes 1492480 | tf_op jit(solution)/shard_map/while/body/eval_jaxpr/dot_general | solution.py:62
  175.4 1.2 fusion.61
  176.6 1.7 constant_dynamic-slice_fusion.11
  181.4 1.3 copy_dynamic-update-slice_fusion.4
  182.7 2.8 %fusion.66 = f32[512,2560]{1,0:T(8,128)} fusion(f32[512,2560]{1,0:T(8,128)} %get-tuple-element.518, s32[]{:T(128)S(6)} %select_n.149, f32[96,512]{1,0:T(8,128)S(1)} %get-tuple-element.493, f32[96,512]{1,0:T(8,128)S(1)} %fusion.64, f32[]{:T(128)} %bitcast.109, bf16[96,2560]{1,0:T(8,128)(2,1)S(1)} %get-tuple-element.545), kind=kOutput, calls=%fused_computation.6.clone.1 | convolution fusion | flops 25444352 | bytes 1492480 | tf_op jit(solution)/shard_map/while/body/eval_jaxpr/dot_general | solution.py:62
  187.7 1.2 fusion.61
  188.9 1.7 constant_dynamic-slice_fusion.11
  193.7 1.3 copy_dynamic-update-slice_fusion.4
  195.0 2.8 %fusion.66 = f32[512,2560]{1,0:T(8,128)} fusion(f32[512,2560]{1,0:T(8,128)} %get-tuple-element.518, s32[]{:T(128)S(6)} %select_n.149, f32[96,512]{1,0:T(8,128)S(1)} %get-tuple-element.493, f32[96,512]{1,0:T(8,128)S(1)} %fusion.64, f32[]{:T(128)} %bitcast.109, bf16[96,2560]{1,0:T(8,128)(2,1)S(1)} %get-tuple-element.545), kind=kOutput, calls=%fused_computation.6.clone.1 | convolution fusion | flops 25444352 | bytes 1492480 | tf_op jit(solution)/shard_map/while/body/eval_jaxpr/dot_general | solution.py:62
  200.0 1.2 fusion.61
  201.2 1.6 constant_dynamic-slice_fusion.11
  205.9 1.2 copy_dynamic-update-slice_fusion.4
  207.2 2.8 %fusion.66 = f32[512,2560]{1,0:T(8,128)} fusion(f32[512,2560]{1,0:T(8,128)} %get-tuple-element.518, s32[]{:T(128)S(6)} %select_n.149, f32[96,512]{1,0:T(8,128)S(1)} %get-tuple-element.493, f32[96,512]{1,0:T(8,128)S(1)} %fusion.64, f32[]{:T(128)} %bitcast.109, bf16[96,2560]{1,0:T(8,128)(2,1)S(1)} %get-tuple-element.545), kind=kOutput, calls=%fused_computation.6.clone.1 | convolution fusion | flops 25444352 | bytes 1492480 | tf_op jit(solution)/shard_map/while/body/eval_jaxpr/dot_general | solution.py:62
  210.0 6.6 %all-to-all-start.2 = ((f32[96,2,1280]{2,1,0:T(2,128)}), f32[96,2,1280]{2,1,0:T(2,128)S(1)}, u32[]{:S(2)}, u32[]{:S(2)}) async-start(f32[96,2,1280]{2,1,0:T(2,128)} %get-tuple-element.205), calls=%async_computation.2 | async-start | bytes 1966080 | tf_op jit(solution)/shard_map/all_to_all | solution.py:172
  216.8 5.9 %convert_element_type.46 = bf16[512,2,1280]{2,1,0:T(2,128)(2,1)} convert(f32[512,2,1280]{2,1,0:T(2,128)} %get-tuple-element.206) | non-fusion elementwise | flops 1310720 | bytes 7864320 | tf_op jit(solution)/shard_map/convert_element_type | solution.py:180
  222.7 1.8 convert_element_type.47
  224.5 15.7 %all-to-all-done.2 = f32[96,2,1280]{2,1,0:T(2,128)S(1)} async-done(((f32[96,2,1280]{2,1,0:T(2,128)}), f32[96,2,1280]{2,1,0:T(2,128)S(1)}, u32[]{:S(2)}, u32[]{:S(2)}) %all-to-all-start.2) | async-done | bytes 983072 | tf_op jit(solution)/shard_map/all_to_all | solution.py:172
  (223 shorter events, 47.5 us)
Async XLA Ops:
  0.6 15.0 %copy-start = (bf16[8,2,1280]{2,1,0:T(2,128)(2,1)S(1)}, bf16[8,2,1280]{2,1,0:T(2,128)(2,1)}, u32[]{:S(2)}) copy-start(bf16[8,2,1280]{2,1,0:T(2,128)(2,1)} %param.14) | copy-start | bytes 122884
  0.6 14.6 %copy-start.5 = (s32[16]{0:T(128)S(1)}, s32[16]{0:T(128)}, u32[]{:S(2)}) copy-start(s32[16]{0:T(128)} %param.22) | copy-start | bytes 196
  0.7 14.4 %copy-start.3 = (s32[16,12]{1,0:T(8,128)S(1)}, s32[16,12]{1,0:T(8,128)}, u32[]{:S(2)}) copy-start(s32[16,12]{1,0:T(8,128)} %param.21) | copy-start | bytes 2308
  0.7 14.8 %copy-start.1 = (bf16[8,2560]{1,0:T(8,128)(2,1)S(1)}, bf16[8,2560]{1,0:T(8,128)(2,1)}, u32[]{:S(2)}) copy-start(bf16[8,2560]{1,0:T(8,128)(2,1)} %param.18) | copy-start | bytes 122884
  0.7 14.6 %copy-start.6 = (f32[10]{0:T(128)S(1)}, f32[10]{0:T(128)}, u32[]{:S(2)}) copy-start(f32[10]{0:T(128)} %param.20) | copy-start | bytes 124
  0.7 14.8 %copy-start.2 = (bf16[8,2,2560]{2,1,0:T(2,128)(2,1)S(1)}, bf16[8,2,2560]{2,1,0:T(2,128)(2,1)}, u32[]{:S(2)}) copy-start(bf16[8,2,2560]{2,1,0:T(2,128)(2,1)} %param.17) | copy-start | bytes 245764
  5.0 31.4 %copy-start.4 = (f32[8,2,10]{2,1,0:T(2,128)S(1)}, f32[8,2,10]{2,1,0:T(2,128)}, u32[]{:S(2)}) copy-start(f32[8,2,10]{2,1,0:T(2,128)} %param.19) | copy-start | bytes 1924
  8.4 23.5 %all-to-all-start.1 = ((bf16[16,6,2560]{2,1,0:T(8,128)(2,1)}), bf16[16,6,2560]{2,1,0:T(8,128)(2,1)S(1)}, u32[]{:S(2)}, u32[]{:S(2)}) async-start(bf16[16,6,2560]{2,1,0:T(8,128)(2,1)} %broadcast_select_fusion.1), calls=%async_computation.1 | async-start | bytes 1310720 | tf_op jit(solution)/shard_map/all_to_all | solution.py:155
  31.9 47.4 %all-to-all-start = ((bf16[96,2,1280]{2,1,0:T(2,128)(2,1)}), bf16[96,2,1280]{2,1,0:T(2,128)(2,1)S(1)}, u32[]{:S(2)}, u32[]{:S(2)}) async-start(bf16[96,2,1280]{2,1,0:T(2,128)(2,1)} %broadcast_select_fusion), calls=%async_computation | async-start | bytes 983040 | tf_op jit(solution)/shard_map/all_to_all | solution.py:154
  210.0 12.7 %slice-start = ((s8[5242880]{0:T(1024)(128)(4,1)}), s8[1048576]{0:T(1024)(128)(4,1)S(1)}, s32[]{:S(2)}) async-start(s8[5242880]{0:T(1024)(128)(4,1)} %bitcast.112), calls=%async_computation.3 | async-start | bytes 2097152
  210.0 30.2 %all-to-all-start.2 = ((f32[96,2,1280]{2,1,0:T(2,128)}), f32[96,2,1280]{2,1,0:T(2,128)S(1)}, u32[]{:S(2)}, u32[]{:S(2)}) async-start(f32[96,2,1280]{2,1,0:T(2,128)} %get-tuple-element.205), calls=%async_computation.2 | async-start | bytes 1966080 | tf_op jit(solution)/shard_map/all_to_all | solution.py:172
  216.8 5.9 %slice-start.1 = ((s8[5242880]{0:T(1024)(128)(4,1)}), s8[4194304]{0:T(1024)(128)(4,1)S(1)}, s32[]{:S(2)}) async-start(s8[5242880]{0:T(1024)(128)(4,1)} %bitcast.112), calls=%async_computation.4 | async-start | bytes 8388608
where the time goes:
time: 246 us; the launch traced here: 243 us
  local copies, waits for them, and re-layouts  74.1 us (30%)
  matrix products  52.4 us (21%)
  blocking collectives  40.9 us (17%)
  waiting for transfers between devices  28.9 us (12%)
  other arithmetic  19.5 us (8%)
  starting transfers between devices  17.7 us (7%)
  loops' own time  7.6 us (3%)
    dot_general x10, matrix products, head_step(): jnp.dot(mixed_weight.T, g_head, preferred_element_type=jnp.float32)  28 us
    all_gather x1, blocking collectives, per_device(): lax.all_gather(log_norms, 'tokens', axis=0, tiled=True)  23.7 us
    all_gather x1, blocking collectives, per_device(): lax.all_gather(slopes, 'tokens', axis=0, tiled=True)  17.2 us
    slice x10, local copies, waits for them, and re-layouts, head_step(): k_head[:, 0]  16.7 us
    all_to_all x1, waiting for transfers between devices, per_device(): lax.all_to_all(query_part, 'tokens', split_axis=0, concat_axis=0, tiled=T...  15.7 us
    all_to_all x1, waiting for transfers between devices, per_device(): lax.all_to_all(sent_grad, 'tokens', split_axis=0, concat_axis=0, tiled=True)  13.2 us
    dynamic_update_slice x10, local copies, waits for them, and re-layouts, head_step(): lax.dynamic_update_slice_in_dim(key_total, key_old + key_new, head_index...  12.7 us
    dot_general x10, matrix products, head_step(): spread = jnp.dot(g_head, v_head.T, preferred_element_type=jnp.float32)  11.6 us
  transfers between devices with their start and end apart: 3, of which 2 were waited for; matrix products, arithmetic and copies ran while one was open for 5% of the time, Pallas kernels for 0%

commit v1 on v0

--- a/solution.py
+++ b/solution.py
@@ -120,8 +120,22 @@
     outs_wide = forward_out.astype(jnp.float32).reshape(text_rows, 2, head_count, value_size)
     map_coefs = jnp.stack([jnp.ones_like(lambdas), -lambdas])
     slopes = jnp.sum(grads_wide[:, None] * outs_wide, axis=3) * map_coefs[None]
+
+    def _lift_ratios(vector, group_axis):
+        then = lax.axis_size(group_axis)
+        reached = lax.axis_index(group_axis)
+        arr_now, found_now = (then, reached)
+        w2, item_now = (vector, 1)
+        while item_now < arr_now:
+            even = lax.ppermute(w2, group_axis, [(d, d ^ item_now) for d in range(arr_now)])
+            outcome_arr = jnp.concatenate([w2, even], axis=0)
+            d_next = jnp.concatenate([even, w2], 0)
+            w2 = jnp.where(found_now & item_now == 0, outcome_arr, d_next)
+            item_now = 2 * item_now
+        return w2
+
     all_norms, all_slopes = (
-        lax.all_gather(log_norms, "tokens", axis=0, tiled=True),
+        _lift_ratios(log_norms, "tokens"),
         lax.all_gather(slopes, "tokens", axis=0, tiled=True),
     )
     zero_keys = jnp.zeros(frame_key.shape, jnp.float32)

time: 246 us -> 228 us (0.927)
  blocking collectives: 40.9 us -> 21.8 us
    all_gather x1 -> x0, blocking collectives: 23.7 us -> none  [per_device(): lax.all_gather(log_norms, 'tokens', axis=0, tiled=True)]
    all_gather x1, blocking collectives: 17.2 us -> 21.8 us  [per_device(): lax.all_gather(slopes, 'tokens', axis=0, tiled=True)]
    ppermute x0 -> x4, starting transfers between devices: none -> 4.15 us  [_lift_ratios(): lax.ppermute(w2, group_axis, [(d, d ^ item_now) for d in range(arr_now)])]
    all_to_all x1, waiting for transfers between devices: 13.2 us -> 9.69 us  [per_device(): lax.all_to_all(sent_grad, 'tokens', split_axis=0, concat_axis=0, tiled=True)]
  transfers between devices with their start and end apart: 3 -> 7, of which waited for: 2 -> 3; matrix products, arithmetic and copies ran while one was open for 5% -> 9% of each run, Pallas kernels for 0% -> 0%
where the time goes in v1:
time: 228 us; the launch traced here: 226 us
  local copies, waits for them, and re-layouts  75.3 us (33%)
  matrix products  52.4 us (23%)
  waiting for transfers between devices  27.3 us (12%)
  blocking collectives  21.8 us (10%)
  other arithmetic  19.9 us (9%)
  starting transfers between devices  19.3 us (8%)
  loops' own time  7.61 us (3%)
    dot_general x10, matrix products, head_step(): jnp.dot(mixed_weight.T, g_head, preferred_element_type=jnp.float32)  28.1 us
    all_gather x1, blocking collectives, per_device(): lax.all_gather(slopes, 'tokens', axis=0, tiled=True)  21.8 us
    slice x10, local copies, waits for them, and re-layouts, head_step(): k_head[:, 0]  16.7 us
    all_to_all x1, waiting for transfers between devices, per_device(): lax.all_to_all(query_part, 'tokens', split_axis=0, concat_axis=0, tiled=T...  15.7 us
    dynamic_update_slice x10, local copies, waits for them, and re-layouts, head_step(): lax.dynamic_update_slice_in_dim(key_total, key_old + key_new, head_index...  12.7 us
    dot_general x10, matrix products, head_step(): spread = jnp.dot(g_head, v_head.T, preferred_element_type=jnp.float32)  11.6 us
    dynamic_slice x10, local copies, waits for them, and re-layouts, head_step(): lax.dynamic_slice_in_dim(key_total, head_index * key_size, key_size, 2)  10.8 us
    all_to_all x1, waiting for transfers between devices, per_device(): lax.all_to_all(sent_grad, 'tokens', split_axis=0, concat_axis=0, tiled=True)  9.69 us
  transfers between devices with their start and end apart: 7, of which 3 were waited for; matrix products, arithmetic and copies ran while one was open for 9% of the time, Pallas kernels for 0%

profile of v1, /device:TPU:9, one launch (start us, length us, event | category | flops | bytes accessed | tf_op | source)
XLA Modules:
  0.0 225.9 jit_solution(8189305380275012512)
XLA Ops:
  2.9 1.2 dynamic_slice.74
  6.5 2.1 gather_fusion.1
  9.9 6.0 %all-to-all-start.1 = ((bf16[16,6,2560]{2,1,0:T(8,128)(2,1)}), bf16[16,6,2560]{2,1,0:T(8,128)(2,1)S(1)}, u32[]{:S(2)}, u32[]{:S(2)}) async-start(bf16[16,6,2560]{2,1,0:T(8,128)(2,1)} %broadcast_select_fusion.1), calls=%async_computation.1 | async-start | bytes 1310720 | tf_op jit(solution)/shard_map/all_to_all | solution.py:169
  16.3 1.6 gather_fusion
  18.0 1.3 broadcast_select_fusion
  19.7 1.2 collective-permute-start.1
  21.0 2.0 collective-permute-done.1
  23.1 9.7 %all-to-all-done.1 = bf16[16,6,2560]{2,1,0:T(8,128)(2,1)S(1)} async-done(((bf16[16,6,2560]{2,1,0:T(8,128)(2,1)}), bf16[16,6,2560]{2,1,0:T(8,128)(2,1)S(1)}, u32[]{:S(2)}, u32[]{:S(2)}) %all-to-all-start.1) | async-done | bytes 491552 | tf_op jit(solution)/shard_map/all_to_all | solution.py:169
  32.8 4.5 %all-to-all-start = ((bf16[96,2,1280]{2,1,0:T(2,128)(2,1)}), bf16[96,2,1280]{2,1,0:T(2,128)(2,1)S(1)}, u32[]{:S(2)}, u32[]{:S(2)}) async-start(bf16[96,2,1280]{2,1,0:T(2,128)(2,1)} %broadcast_select_fusion), calls=%async_computation | async-start | bytes 983040 | tf_op jit(solution)/shard_map/all_to_all | solution.py:168
  37.4 2.2 collective-permute-start.3
  39.6 21.8 %all_gather.3 = f32[128,2,10]{2,1,0:T(2,128)S(1)} all-gather(f32[8,2,10]{2,1,0:T(2,128)S(1)} %copy.71), channel_id=1, replica_groups=mesh['groups'=2,'tokens'=16] {'tokens'}, dimensions={0}, use_global_device_ids=true | all-gather | bytes 10880 | tf_op jit(solution)/shard_map/all_gather | solution.py:139
  63.7 1.2 broadcast_in_dim.73.clone
  65.0 3.0 %broadcast_in_dim.72 = f32[512,2560]{1,0:T(8,128)} broadcast(f32[]{:T(128)} %constant.129.clone.1), dimensions={} | broadcast | bytes 5242884 | tf_op jit(solution)/shard_map/broadcast_in_dim | solution.py:142
  68.0 3.7 %broadcast_in_dim.71.clone = f32[512,2,1280]{2,1,0:T(2,128)} broadcast(f32[]{:T(128)} %constant.129.clone.1), dimensions={} | broadcast | bytes 5242884 | tf_op jit(solution)/shard_map/broadcast_in_dim | solution.py:141
  71.6 122.9 %while.18 = (s32[]{:T(128)}, f32[512,2,1280]{2,1,0:T(2,128)}, f32[512,2560]{1,0:T(8,128)}, f32[96,2,1280]{2,1,0:T(2,128)}, bf16[96,2,1280]{2,1,0:T(2,128)(2,1)S(...) while((s32[]{:T(128)}, f32[512,2,1280]{2,1,0:T(2,128)}, ...), condition=%wide.region_6.8_spmd.clone, body=%wide.region_5.7_spmd.clone.sunk | while | flops 127189576 | bytes 9318833 | solution.py:97
  73.9 1.2 fusion.61
  75.0 1.6 constant_dynamic-slice_fusion.11
  77.9 1.1 constant_dynamic-slice_fusion.13
  79.8 1.3 copy_dynamic-update-slice_fusion.4
  81.1 2.8 %fusion.66 = f32[512,2560]{1,0:T(8,128)} fusion(f32[512,2560]{1,0:T(8,128)} %get-tuple-element.520, s32[]{:T(128)S(6)} %select_n.197, f32[96,512]{1,0:T(8,128)S(1)} %get-tuple-element.495, f32[96,512]{1,0:T(8,128)S(1)} %fusion.64, f32[]{:T(128)} %bitcast.112, bf16[96,2560]{1,0:T(8,128)(2,1)S(1)} %get-tuple-element.547), kind=kOutput, calls=%fused_computation.6.clone.1 | convolution fusion | flops 25444352 | bytes 1492480 | tf_op jit(solution)/shard_map/while/body/eval_jaxpr/dot_general | solution.py:62
  86.1 1.2 fusion.61
  87.3 1.6 constant_dynamic-slice_fusion.11
  90.1 1.1 constant_dynamic-slice_fusion.13
  92.0 1.3 copy_dynamic-update-slice_fusion.4
  93.3 2.8 %fusion.66 = f32[512,2560]{1,0:T(8,128)} fusion(f32[512,2560]{1,0:T(8,128)} %get-tuple-element.520, s32[]{:T(128)S(6)} %select_n.197, f32[96,512]{1,0:T(8,128)S(1)} %get-tuple-element.495, f32[96,512]{1,0:T(8,128)S(1)} %fusion.64, f32[]{:T(128)} %bitcast.112, bf16[96,2560]{1,0:T(8,128)(2,1)S(1)} %get-tuple-element.547), kind=kOutput, calls=%fused_computation.6.clone.1 | convolution fusion | flops 25444352 | bytes 1492480 | tf_op jit(solution)/shard_map/while/body/eval_jaxpr/dot_general | solution.py:62
  98.4 1.2 fusion.61
  99.6 1.7 constant_dynamic-slice_fusion.11
  102.5 1.1 constant_dynamic-slice_fusion.13
  104.4 1.3 copy_dynamic-update-slice_fusion.4
  105.7 2.8 %fusion.66 = f32[512,2560]{1,0:T(8,128)} fusion(f32[512,2560]{1,0:T(8,128)} %get-tuple-element.520, s32[]{:T(128)S(6)} %select_n.197, f32[96,512]{1,0:T(8,128)S(1)} %get-tuple-element.495, f32[96,512]{1,0:T(8,128)S(1)} %fusion.64, f32[]{:T(128)} %bitcast.112, bf16[96,2560]{1,0:T(8,128)(2,1)S(1)} %get-tuple-element.547), kind=kOutput, calls=%fused_computation.6.clone.1 | convolution fusion | flops 25444352 | bytes 1492480 | tf_op jit(solution)/shard_map/while/body/eval_jaxpr/dot_general | solution.py:62
  110.7 1.2 fusion.61
  111.9 1.7 constant_dynamic-slice_fusion.11
  116.7 1.3 copy_dynamic-update-slice_fusion.4
  118.0 2.9 %fusion.66 = f32[512,2560]{1,0:T(8,128)} fusion(f32[512,2560]{1,0:T(8,128)} %get-tuple-element.520, s32[]{:T(128)S(6)} %select_n.197, f32[96,512]{1,0:T(8,128)S(1)} %get-tuple-element.495, f32[96,512]{1,0:T(8,128)S(1)} %fusion.64, f32[]{:T(128)} %bitcast.112, bf16[96,2560]{1,0:T(8,128)(2,1)S(1)} %get-tuple-element.547), kind=kOutput, calls=%fused_computation.6.clone.1 | convolution fusion | flops 25444352 | bytes 1492480 | tf_op jit(solution)/shard_map/while/body/eval_jaxpr/dot_general | solution.py:62
  123.1 1.2 fusion.61
  124.3 1.6 constant_dynamic-slice_fusion.11
  129.0 1.3 copy_dynamic-update-slice_fusion.4
  130.3 2.8 %fusion.66 = f32[512,2560]{1,0:T(8,128)} fusion(f32[512,2560]{1,0:T(8,128)} %get-tuple-element.520, s32[]{:T(128)S(6)} %select_n.197, f32[96,512]{1,0:T(8,128)S(1)} %get-tuple-element.495, f32[96,512]{1,0:T(8,128)S(1)} %fusion.64, f32[]{:T(128)} %bitcast.112, bf16[96,2560]{1,0:T(8,128)(2,1)S(1)} %get-tuple-element.547), kind=kOutput, calls=%fused_computation.6.clone.1 | convolution fusion | flops 25444352 | bytes 1492480 | tf_op jit(solution)/shard_map/while/body/eval_jaxpr/dot_general | solution.py:62
  135.3 1.2 fusion.61
  136.5 1.7 constant_dynamic-slice_fusion.11
  141.3 1.2 copy_dynamic-update-slice_fusion.4
  142.5 2.8 %fusion.66 = f32[512,2560]{1,0:T(8,128)} fusion(f32[512,2560]{1,0:T(8,128)} %get-tuple-element.520, s32[]{:T(128)S(6)} %select_n.197, f32[96,512]{1,0:T(8,128)S(1)} %get-tuple-element.495, f32[96,512]{1,0:T(8,128)S(1)} %fusion.64, f32[]{:T(128)} %bitcast.112, bf16[96,2560]{1,0:T(8,128)(2,1)S(1)} %get-tuple-element.547), kind=kOutput, calls=%fused_computation.6.clone.1 | convolution fusion | flops 25444352 | bytes 1492480 | tf_op jit(solution)/shard_map/while/body/eval_jaxpr/dot_general | solution.py:62
  147.6 1.2 fusion.61
  148.7 1.7 constant_dynamic-slice_fusion.11
  153.5 1.3 copy_dynamic-update-slice_fusion.4
  154.8 2.8 %fusion.66 = f32[512,2560]{1,0:T(8,128)} fusion(f32[512,2560]{1,0:T(8,128)} %get-tuple-element.520, s32[]{:T(128)S(6)} %select_n.197, f32[96,512]{1,0:T(8,128)S(1)} %get-tuple-element.495, f32[96,512]{1,0:T(8,128)S(1)} %fusion.64, f32[]{:T(128)} %bitcast.112, bf16[96,2560]{1,0:T(8,128)(2,1)S(1)} %get-tuple-element.547), kind=kOutput, calls=%fused_computation.6.clone.1 | convolution fusion | flops 25444352 | bytes 1492480 | tf_op jit(solution)/shard_map/while/body/eval_jaxpr/dot_general | solution.py:62
  159.8 1.2 fusion.61
  161.0 1.7 constant_dynamic-slice_fusion.11
  164.0 1.1 constant_dynamic-slice_fusion.13
  165.9 1.3 copy_dynamic-update-slice_fusion.4
  167.2 2.8 %fusion.66 = f32[512,2560]{1,0:T(8,128)} fusion(f32[512,2560]{1,0:T(8,128)} %get-tuple-element.520, s32[]{:T(128)S(6)} %select_n.197, f32[96,512]{1,0:T(8,128)S(1)} %get-tuple-element.495, f32[96,512]{1,0:T(8,128)S(1)} %fusion.64, f32[]{:T(128)} %bitcast.112, bf16[96,2560]{1,0:T(8,128)(2,1)S(1)} %get-tuple-element.547), kind=kOutput, calls=%fused_computation.6.clone.1 | convolution fusion | flops 25444352 | bytes 1492480 | tf_op jit(solution)/shard_map/while/body/eval_jaxpr/dot_general | solution.py:62
  172.2 1.2 fusion.61
  173.4 1.7 constant_dynamic-slice_fusion.11
  176.3 1.1 constant_dynamic-slice_fusion.13
  178.2 1.3 copy_dynamic-update-slice_fusion.4
  179.5 2.8 %fusion.66 = f32[512,2560]{1,0:T(8,128)} fusion(f32[512,2560]{1,0:T(8,128)} %get-tuple-element.520, s32[]{:T(128)S(6)} %select_n.197, f32[96,512]{1,0:T(8,128)S(1)} %get-tuple-element.495, f32[96,512]{1,0:T(8,128)S(1)} %fusion.64, f32[]{:T(128)} %bitcast.112, bf16[96,2560]{1,0:T(8,128)(2,1)S(1)} %get-tuple-element.547), kind=kOutput, calls=%fused_computation.6.clone.1 | convolution fusion | flops 25444352 | bytes 1492480 | tf_op jit(solution)/shard_map/while/body/eval_jaxpr/dot_general | solution.py:62
  184.5 1.2 fusion.61
  185.7 1.6 constant_dynamic-slice_fusion.11
  190.5 1.3 copy_dynamic-update-slice_fusion.4
  191.8 2.8 %fusion.66 = f32[512,2560]{1,0:T(8,128)} fusion(f32[512,2560]{1,0:T(8,128)} %get-tuple-element.520, s32[]{:T(128)S(6)} %select_n.197, f32[96,512]{1,0:T(8,128)S(1)} %get-tuple-element.495, f32[96,512]{1,0:T(8,128)S(1)} %fusion.64, f32[]{:T(128)} %bitcast.112, bf16[96,2560]{1,0:T(8,128)(2,1)S(1)} %get-tuple-element.547), kind=kOutput, calls=%fused_computation.6.clone.1 | convolution fusion | flops 25444352 | bytes 1492480 | tf_op jit(solution)/shard_map/while/body/eval_jaxpr/dot_general | solution.py:62
  194.5 4.6 %all-to-all-start.2 = ((f32[96,2,1280]{2,1,0:T(2,128)}), f32[96,2,1280]{2,1,0:T(2,128)S(1)}, u32[]{:S(2)}, u32[]{:S(2)}) async-start(f32[96,2,1280]{2,1,0:T(2,128)} %get-tuple-element.205), calls=%async_computation.2 | async-start | bytes 1966080 | tf_op jit(solution)/shard_map/all_to_all | solution.py:186
  199.3 5.9 %convert_element_type.46 = bf16[512,2,1280]{2,1,0:T(2,128)(2,1)} convert(f32[512,2,1280]{2,1,0:T(2,128)} %get-tuple-element.206) | non-fusion elementwise | flops 1310720 | bytes 7864320 | tf_op jit(solution)/shard_map/convert_element_type | solution.py:194
  205.3 1.8 convert_element_type.47
  207.1 15.7 %all-to-all-done.2 = f32[96,2,1280]{2,1,0:T(2,128)S(1)} async-done(((f32[96,2,1280]{2,1,0:T(2,128)}), f32[96,2,1280]{2,1,0:T(2,128)S(1)}, u32[]{:S(2)}, u32[]{:S(2)}) %all-to-all-start.2) | async-done | bytes 983072 | tf_op jit(solution)/shard_map/all_to_all | solution.py:186
  (236 shorter events, 51.9 us)
Async XLA Ops:
  0.6 15.7 %copy-start = (bf16[8,2,1280]{2,1,0:T(2,128)(2,1)S(1)}, bf16[8,2,1280]{2,1,0:T(2,128)(2,1)}, u32[]{:S(2)}) copy-start(bf16[8,2,1280]{2,1,0:T(2,128)(2,1)} %param.14) | copy-start | bytes 122884
  0.6 17.3 %copy-start.4 = (s32[16]{0:T(128)S(1)}, s32[16]{0:T(128)}, u32[]{:S(2)}) copy-start(s32[16]{0:T(128)} %param.22) | copy-start | bytes 196
  0.7 15.2 %copy-start.3 = (s32[16,12]{1,0:T(8,128)S(1)}, s32[16,12]{1,0:T(8,128)}, u32[]{:S(2)}) copy-start(s32[16,12]{1,0:T(8,128)} %param.21) | copy-start | bytes 2308
  0.7 15.6 %copy-start.1 = (bf16[8,2560]{1,0:T(8,128)(2,1)S(1)}, bf16[8,2560]{1,0:T(8,128)(2,1)}, u32[]{:S(2)}) copy-start(bf16[8,2560]{1,0:T(8,128)(2,1)} %param.18) | copy-start | bytes 122884
  0.7 15.5 %copy-start.5 = (f32[10]{0:T(128)S(1)}, f32[10]{0:T(128)}, u32[]{:S(2)}) copy-start(f32[10]{0:T(128)} %param.20) | copy-start | bytes 124
  0.7 15.6 %copy-start.2 = (bf16[8,2,2560]{2,1,0:T(2,128)(2,1)S(1)}, bf16[8,2,2560]{2,1,0:T(2,128)(2,1)}, u32[]{:S(2)}) copy-start(bf16[8,2,2560]{2,1,0:T(2,128)(2,1)} %param.17) | copy-start | bytes 245764
  1.5 18.1 %collective-permute-start = (f32[8,2,10]{0,1,2:T(2,128)S(1)}, f32[8,2,10]{0,1,2:T(2,128)S(1)}, u32[]{:S(2)}, u32[]{:S(2)}) collective-permute-start(f32[8,2,10]{0,1,2:T(2,128)S(1)} %copy.65), channel_id=1, source_target_pairs={{0,1},{1,0},{2,3},{3,2},{4,5},{5,4},{6,7},{7,6},{8,9},{9,8},{10,11... | collective-permute-start | bytes 1928 | tf_op jit(solution)/shard_map/ppermute | solution.py:130
  9.9 22.9 %all-to-all-start.1 = ((bf16[16,6,2560]{2,1,0:T(8,128)(2,1)}), bf16[16,6,2560]{2,1,0:T(8,128)(2,1)S(1)}, u32[]{:S(2)}, u32[]{:S(2)}) async-start(bf16[16,6,2560]{2,1,0:T(8,128)(2,1)} %broadcast_select_fusion.1), calls=%async_computation.1 | async-start | bytes 1310720 | tf_op jit(solution)/shard_map/all_to_all | solution.py:169
  19.7 3.2 %collective-permute-start.1 = (f32[16,2,10]{0,1,2:T(2,128)S(1)}, f32[16,2,10]{0,1,2:T(2,128)S(1)}, u32[]{:S(2)}, u32[]{:S(2)}) collective-permute-start(f32[16,2,10]{0,1,2:T(2,128)S(1)} %maximum_select_fusion), channel_id=1, source_target_pairs={{0,2},{1,3},{2,0},{3,1},{4,6},{5,7},{6,4},{7,5},{8,10},{9,11},{10,... | collective-permute-start | bytes 3848 | tf_op jit(solution)/shard_map/ppermute | solution.py:130
  23.0 14.3 %collective-permute-start.2 = (f32[32,2,10]{0,1,2:T(2,128)S(1)}, f32[32,2,10]{0,1,2:T(2,128)S(1)}, u32[]{:S(2)}, u32[]{:S(2)}) collective-permute-start(f32[32,2,10]{0,1,2:T(2,128)S(1)} %maximum_select_fusion.1), channel_id=1, source_target_pairs={{0,4},{1,5},{2,6},{3,7},{4,0},{5,1},{6,2},{7,3},{8,12},{9,13},{10,... | collective-permute-start | bytes 7688 | tf_op jit(solution)/shard_map/ppermute | solution.py:130
  32.8 30.9 %all-to-all-start = ((bf16[96,2,1280]{2,1,0:T(2,128)(2,1)}), bf16[96,2,1280]{2,1,0:T(2,128)(2,1)S(1)}, u32[]{:S(2)}, u32[]{:S(2)}) async-start(bf16[96,2,1280]{2,1,0:T(2,128)(2,1)} %broadcast_select_fusion), calls=%async_computation | async-start | bytes 983040 | tf_op jit(solution)/shard_map/all_to_all | solution.py:168
  37.4 24.7 %collective-permute-start.3 = (f32[64,2,10]{0,1,2:T(2,128)S(1)}, f32[64,2,10]{0,1,2:T(2,128)S(1)}, u32[]{:S(2)}, u32[]{:S(2)}) collective-permute-start(f32[64,2,10]{0,1,2:T(2,128)S(1)} %maximum_select_fusion.2), channel_id=1, source_target_pairs={{0,8},{1,9},{2,10},{3,11},{4,12},{5,13},{6,14},{7,15},{8,0},{9,1},... | collective-permute-start | bytes 15368 | tf_op jit(solution)/shard_map/ppermute | solution.py:130
  194.5 10.7 %slice-start = ((s8[5242880]{0:T(1024)(128)(4,1)}), s8[1048576]{0:T(1024)(128)(4,1)S(1)}, s32[]{:S(2)}) async-start(s8[5242880]{0:T(1024)(128)(4,1)} %bitcast.115), calls=%async_computation.3 | async-start | bytes 2097152
  194.5 28.2 %all-to-all-start.2 = ((f32[96,2,1280]{2,1,0:T(2,128)}), f32[96,2,1280]{2,1,0:T(2,128)S(1)}, u32[]{:S(2)}, u32[]{:S(2)}) async-start(f32[96,2,1280]{2,1,0:T(2,128)} %get-tuple-element.205), calls=%async_computation.2 | async-start | bytes 1966080 | tf_op jit(solution)/shard_map/all_to_all | solution.py:186
  199.3 5.9 %slice-start.1 = ((s8[5242880]{0:T(1024)(128)(4,1)}), s8[4194304]{0:T(1024)(128)(4,1)S(1)}, s32[]{:S(2)}) async-start(s8[5242880]{0:T(1024)(128)(4,1)} %bitcast.115), calls=%async_computation.4 | async-start | bytes 8388608
